TPU v7x, 32 devices: a whole 2x2x4 slice. The times are simulated.
32 devices in a mesh: layer: 4 (over y, core), shard: 8 (over z, x).
Axes of the slice: x: 2, y: 2, z: 4, core: 2. Of those that a mesh axis runs over, the one named last changes fastest.
Arguments:
- input_acts: bfloat16 [8, 4096, 5120], P('layer', 'shard'), may hold values from -6 to 6
- output_grads: bfloat16 [8, 4096, 1024], P('layer', 'shard'), may hold values from -6 to 6
- input_inverse: bfloat16 [8, 5120, 5120], P('layer', 'shard'), may hold values from -1 to 2, as said below
- output_inverse: bfloat16 [8, 1024, 1024], P('layer', 'shard'), may hold values from -1 to 2, as said below
- query_input: bfloat16 [8, 5120, 512], P(None, 'shard'), may hold values from -0.0048828125 to 0.0048828125
- query_output: bfloat16 [8, 1024, 512], P(None, 'shard'), may hold values from -0.1875 to 0.1875
- layer_order: int32 [8], replicated, may hold values from 0 to 7, each once
Outputs:
- scores: float32 [4096, 16], P('shard', 'layer')
Inputs may be any that keep to these rules, and one draw needn't show every extreme that they name: `input_inverse`: symmetric in its last two dimensions, with a unit-sized diagonal. `output_inverse`: symmetric in its last two dimensions, with a unit-sized diagonal.
All inputs are finite; a program needn't handle non-finite values.
Results may differ from a plain program's by a relative error of at most 0.0045.
Values may be sent and summed in bfloat16 or wider, within the bound.
No kernel may reach another device: no remote copies, remote signals or barrier semaphores. Data moves between devices by JAX's collectives and lax.ppermute only.
A program may use at most 128 MiB of HBM per device.

v0:
```python
import jax
import jax.numpy as jnp
from jax import lax
from jax.sharding import PartitionSpec as P

QUERIES = 16


def shards(
    input_acts, output_grads, input_inverse, output_inverse, query_input, query_output, layer_order
):
    depth = input_acts.shape[0]
    tokens = input_acts.shape[1]
    first = lax.axis_index("layer") * depth
    chosen_in = []
    chosen_out = []
    for position in range(depth):
        model_layer = layer_order[first + position]
        chosen_in.append(lax.dynamic_index_in_dim(query_input, model_layer, 0, keepdims=False))
        chosen_out.append(lax.dynamic_index_in_dim(query_output, model_layer, 0, keepdims=False))
    vectors_in = jnp.stack(chosen_in, axis=1)
    vectors_out = jnp.stack(chosen_out, axis=1)
    width = vectors_in.shape[2]
    whole_in = lax.all_gather(vectors_in, "shard", axis=0, tiled=True)
    folded_in = jnp.einsum(
        "jsk,kjn->sjn", input_inverse, whole_in, preferred_element_type=jnp.float32
    ).astype(jnp.bfloat16)
    columns = input_acts
    left = jnp.einsum(
        "jti,ijn->jtn",
        columns,
        lax.all_gather(folded_in, "shard", axis=0, tiled=True),
        preferred_element_type=jnp.float32,
    )
    whole_out = lax.all_gather(vectors_out, "shard", axis=0, tiled=True)
    folded_out = jnp.einsum(
        "jsk,kjn->sjn", output_inverse, whole_out, preferred_element_type=jnp.float32
    ).astype(jnp.bfloat16)
    columns = output_grads
    right = jnp.einsum(
        "jti,ijn->jtn",
        columns,
        lax.all_gather(folded_out, "shard", axis=0, tiled=True),
        preferred_element_type=jnp.float32,
    )
    product = (left * right).reshape(depth, tokens, QUERIES, width // QUERIES).sum(axis=(0, 3))
    return lax.psum_scatter(product, "layer", scatter_dimension=1, tiled=True)


def solution(mesh):
    in_specs = (
        P("layer", "shard", None),
        P("layer", "shard", None),
        P("layer", "shard", None),
        P("layer", "shard", None),
        P(None, "shard", None),
        P(None, "shard", None),
        P(),
    )
    out_specs = P("shard", "layer")
    return jax.shard_map(shards, mesh=mesh, in_specs=in_specs, out_specs=out_specs, check_vma=False)
```

profile of v0, /device:TPU:0, one launch (start us, length us, event | category | flops | bytes accessed | tf_op | source)
XLA Modules:
  0.0 442.9 jit_solution(11020521583007273015)
XLA Ops:
  6.5 0.0 copy-start
  6.5 0.0 all-gather.5.cloned.1.call-start
  6.5 1.5 fusion.2
  11.8 2.2 constant_dynamic-slice_fusion.3
  14.0 0.3 copy.8
  14.3 1.4 copy.9
  15.7 1.3 pad_maximum_fusion
  17.0 0.0 all-gather.5.cloned.1.call-update
  17.0 0.0 all-gather.9.cloned.1.call-start
  17.1 1.0 constant_dynamic-slice_fusion.1
  18.1 0.1 copy.10
  18.2 0.1 copy.11
  18.3 0.7 pad_maximum_fusion.1
  19.0 0.0 all-gather.9.cloned.1.call-update
  19.1 0.0 copy-start.1
  19.1 0.0 all-gather.7.cloned.1.call-start
  19.1 150.9 %all-gather.5.cloned.1.call-done = bf16[5120,2,512]{0,2,1:T(8,128)(2,1)} async-done(((bf16[640,2,512]{0,2,1:T(8,128)(2,1)}), bf16[5120,2,512]{0,2,1:T(8,128)(2,1)}) %all-gather.5.cloned.1.call-update) | async-done | bytes 10485776 | tf_op jit(solution)/shard_map/all_gather | solution.py:24
  170.0 15.7 %fusion = bf16[640,2,512]{0,2,1:T(8,128)(2,1)} fusion(bf16[5120,2,512]{0,2,1:T(8,128)(2,1)} %all-gather.5.cloned.1.call-done, bf16[2,640,5120]{2,1,0:T(8,128)(2,1)} %param.9), kind=kOutput, calls=%fused_computation.2 | convolution fusion | flops 6711541760 | bytes 24903680 | tf_op jit(solution)/shard_map/jsk,kjn->sjn/dot_general | solution.py:25
  185.7 0.0 copy-start.2
  185.7 0.0 all-gather.7.cloned.1.call-update
  185.7 0.0 all-gather.11.cloned.1.call-start
  185.8 34.8 %all-gather.9.cloned.1.call-done = bf16[1024,2,512]{0,2,1:T(8,128)(2,1)} async-done(((bf16[128,2,512]{0,2,1:T(8,128)(2,1)}), bf16[1024,2,512]{0,2,1:T(8,128)(2,1)}) %all-gather.9.cloned.1.call-update) | async-done | bytes 2097168 | tf_op jit(solution)/shard_map/all_gather | solution.py:35
  220.6 0.0 copy-done.1
  220.6 3.0 fusion.1
  223.6 0.0 all-gather.11.cloned.1.call-update
  223.7 0.0 copy-done.2
  223.7 0.6 dynamic-slice
  224.9 146.3 %all-gather.7.cloned.1.call-done = bf16[5120,2,512]{0,2,1:T(8,128)(2,1)} async-done(((bf16[640,2,512]{0,2,1:T(8,128)(2,1)}), bf16[5120,2,512]{0,2,1:T(8,128)(2,1)}) %all-gather.7.cloned.1.call-update) | async-done | bytes 10485776 | tf_op jit(solution)/shard_map/all_gather | solution.py:32
  371.2 12.4 %fusion.3 = f32[2,512,512]{2,1,0:T(8,128)} fusion(bf16[5120,2,512]{0,2,1:T(8,128)(2,1)} %all-gather.7.cloned.1.call-done, bf16[2,512,5120]{2,1,0:T(8,128)(2,1)} %param.7), kind=kOutput, calls=%fused_computation.14 | convolution fusion | flops 5368709120 | bytes 23068672 | tf_op jit(solution)/shard_map/jti,ijn->jtn/dot_general | solution.py:29
  383.5 38.1 %all-gather.11.cloned.1.call-done = bf16[1024,2,512]{0,2,1:T(8,128)(2,1)} async-done(((bf16[128,2,512]{0,2,1:T(8,128)(2,1)}), bf16[1024,2,512]{0,2,1:T(8,128)(2,1)}) %all-gather.11.cloned.1.call-update) | async-done | bytes 2097168 | tf_op jit(solution)/shard_map/all_gather | solution.py:43
  421.6 0.0 copy-done
  421.6 3.6 multiply_reduce_fusion
  425.2 0.2 bitcast_reduce_fusion
  425.4 10.4 %all-reduce = f32[512,16]{0,1:T(8,128)S(1)} all-reduce(f32[512,16]{0,1:T(8,128)S(1)} %bitcast_reduce_fusion), channel_id=2, replica_groups=mesh['layer'=4,'shard'=8] {'layer'}, use_global_device_ids=true, to_apply=%region_2.3.clone | all-reduce | flops 8192 | bytes 65536
  435.8 0.6 constant_dynamic-slice_fusion.4
Async XLA Ops:
  6.5 415.1 %copy-start = (bf16[2,512,1024]{2,1,0:T(8,128)(2,1)S(1)}, bf16[2,512,1024]{2,1,0:T(8,128)(2,1)}, u32[]{:S(2)}) copy-start(bf16[2,512,1024]{2,1,0:T(8,128)(2,1)} %param.8) | copy-start | bytes 6291460
  6.5 163.5 %all-gather.5.cloned.1.call-start = ((), (), s32[]{:S(2)}) async-start(), calls=%async_computation | async-start | bytes 11796480 | tf_op jit(solution)/shard_map/all_gather | solution.py:24
  17.0 203.6 %all-gather.9.cloned.1.call-start = ((), (), s32[]{:S(2)}) async-start(), calls=%async_computation.2 | async-start | bytes 2359296 | tf_op jit(solution)/shard_map/all_gather | solution.py:35
  19.1 201.5 %copy-start.1 = (bf16[2,128,1024]{2,1,0:T(8,128)(2,1)S(1)}, bf16[2,128,1024]{2,1,0:T(8,128)(2,1)}, u32[]{:S(2)}) copy-start(bf16[2,128,1024]{2,1,0:T(8,128)(2,1)} %param.10) | copy-start | bytes 1572868
  19.1 352.1 %all-gather.7.cloned.1.call-start = ((), (), s32[]{:S(2)}) async-start(), calls=%async_computation.1 | async-start | bytes 11796480 | tf_op jit(solution)/shard_map/all_gather | solution.py:32
  185.7 38.0 %copy-start.2 = (u32[32]{0:T(128)S(1)}, u32[32]{0:T(128)}, u32[]{:S(2)}) copy-start(u32[32]{0:T(128)} %constant.35) | copy-start | bytes 388
  185.7 235.9 %all-gather.11.cloned.1.call-start = ((), (), s32[]{:S(2)}) async-start(), calls=%async_computation.3 | async-start | bytes 2359296 | tf_op jit(solution)/shard_map/all_gather | solution.py:43
Sparse Core Ops, SparseCore 0:
  17.1 152.8 all-gather.4
  172.1 48.5 all-gather.8
  222.8 148.2 all-gather.6
  373.1 48.5 all-gather.10
where the time goes:
time: 443 us
  waiting for transfers between devices  370 us (84%)
  matrix products  34.7 us (8%)
  between operations  17.7 us (4%)
  blocking collectives  10.4 us (2%)
  local copies, waits for them, and re-layouts  7.78 us (2%)
    all_gather x1, waiting for transfers between devices, shards(): whole_in = lax.all_gather(vectors_in, 'shard', axis=0, tiled=True)  151 us
    all_gather x1, waiting for transfers between devices, shards(): lax.all_gather(folded_in, 'shard', axis=0, tiled=True)  146 us
    all_gather x1, waiting for transfers between devices, shards(): lax.all_gather(folded_out, 'shard', axis=0, tiled=True)  38.1 us
    all_gather x1, waiting for transfers between devices, shards(): whole_out = lax.all_gather(vectors_out, 'shard', axis=0, tiled=True)  34.8 us
    dot_general x1, matrix products, shards(): jnp.einsum('jsk,kjn->sjn', input_inverse, whole_in, preferred_element_typ...  15.7 us
    dot_general x1, matrix products, shards(): jnp.einsum('jti,ijn->jtn', columns, lax.all_gather(folded_in, 'shard', ax...  12.4 us
    unnamed x1, blocking collectives  10.4 us
  transfers between devices with their start and end apart: 4, of which 4 were waited for; matrix products, arithmetic and copies ran while one was open for 8% of the time, Pallas kernels for 0%

commit v1 on v0

--- a/solution.py
+++ b/solution.py
@@ -37,12 +37,38 @@
         "jsk,kjn->sjn", output_inverse, whole_out, preferred_element_type=jnp.float32
     ).astype(jnp.bfloat16)
     columns = output_grads
-    right = jnp.einsum(
+    peers, index, rows = (lax.axis_size("shard"), lax.axis_index("shard"), folded_out.shape[0])
+    right_2 = [(i, (i + 1) % peers) for i in range(peers)]
+    left_2 = [(i, (i - 1) % peers) for i in range(peers)]
+    halfway = peers // 2
+    from_left = from_right = folded_out
+    so_far = jnp.einsum(
         "jti,ijn->jtn",
-        columns,
-        lax.all_gather(folded_out, "shard", axis=0, tiled=True),
+        lax.dynamic_slice_in_dim(columns, index * rows, folded_out.shape[0], axis=2),
+        folded_out,
         preferred_element_type=jnp.float32,
     )
+    for step in range(1, halfway + 1):
+        from_left = lax.ppermute(from_left, "shard", right_2)
+        if step < peers - halfway:
+            from_right = lax.ppermute(from_right, "shard", left_2)
+            so_far = so_far + jnp.einsum(
+                "jti,ijn->jtn",
+                lax.dynamic_slice_in_dim(
+                    columns, (index + step) % peers * rows, from_right.shape[0], axis=2
+                ),
+                from_right,
+                preferred_element_type=jnp.float32,
+            )
+        so_far = so_far + jnp.einsum(
+            "jti,ijn->jtn",
+            lax.dynamic_slice_in_dim(
+                columns, (index - step) % peers * rows, from_left.shape[0], axis=2
+            ),
+            from_left,
+            preferred_element_type=jnp.float32,
+        )
+    right = so_far
     product = (left * right).reshape(depth, tokens, QUERIES, width // QUERIES).sum(axis=(0, 3))
     return lax.psum_scatter(product, "layer", scatter_dimension=1, tiled=True)
 

time: 443 us -> 423 us (0.955)
  waiting for transfers between devices: 370 us -> 323 us
  starting transfers between devices: 0.13 us -> 13.7 us
  matrix products: 34.7 us -> 48.2 us
    all_gather x1, waiting for transfers between devices: 146 us -> 108 us  [shards(): lax.all_gather(folded_in, 'shard', axis=0, tiled=True)]
    all_gather x1 -> x0, waiting for transfers between devices: 38.1 us -> none  [shards(): lax.all_gather(folded_out, 'shard', axis=0, tiled=True)]
    ppermute x0 -> x7, waiting for transfers between devices: none -> 30.9 us  [the longest x4 30.3 us: shards(): from_left = lax.ppermute(from_left, 'shard', right_2)]
    dot_general x1 -> x8, matrix products: 3.61 us -> 17.7 us  [the longest x4 10.5 us: shards(): jnp.einsum('jti,ijn->jtn', lax.dynamic_slice_in_dim(columns, (index - ste...]
    ppermute x0 -> x7, starting transfers between devices: none -> 13.6 us  [the longest x3 7.1 us: shards(): from_right = lax.ppermute(from_right, 'shard', left_2)]
  transfers between devices with their start and end apart: 4 -> 10, of which waited for: 4 -> 7; matrix products, arithmetic and copies ran while one was open for 8% -> 11% of each run, Pallas kernels for 0% -> 0%
where the time goes in v1:
time: 423 us
  waiting for transfers between devices  323 us (76%)
  matrix products  48.2 us (11%)
  between operations  17.6 us (4%)
  starting transfers between devices  13.7 us (3%)
  blocking collectives  10.3 us (2%)
  local copies, waits for them, and re-layouts  7.75 us (2%)
    all_gather x1, waiting for transfers between devices, shards(): whole_in = lax.all_gather(vectors_in, 'shard', axis=0, tiled=True)  151 us
    all_gather x1, waiting for transfers between devices, shards(): lax.all_gather(folded_in, 'shard', axis=0, tiled=True)  108 us
    all_gather x1, waiting for transfers between devices, shards(): whole_out = lax.all_gather(vectors_out, 'shard', axis=0, tiled=True)  33.5 us
    ppermute x4, waiting for transfers between devices, shards(): from_left = lax.ppermute(from_left, 'shard', right_2)  30.3 us
    dot_general x1, matrix products, shards(): jnp.einsum('jsk,kjn->sjn', input_inverse, whole_in, preferred_element_typ...  15.7 us
    dot_general x1, matrix products, shards(): jnp.einsum('jti,ijn->jtn', columns, lax.all_gather(folded_in, 'shard', ax...  12.5 us
    dot_general x4, matrix products, shards(): jnp.einsum('jti,ijn->jtn', lax.dynamic_slice_in_dim(columns, (index - ste...  10.5 us
    unnamed x1, blocking collectives  10.3 us
  transfers between devices with their start and end apart: 10, of which 7 were waited for; matrix products, arithmetic and copies ran while one was open for 11% of the time, Pallas kernels for 0%

profile of v1, /device:TPU:0, one launch (start us, length us, event | category | flops | bytes accessed | tf_op | source)
XLA Modules:
  0.0 423.0 jit_solution(2728763809230795024)
XLA Ops:
  6.5 1.4 fusion.26
  11.5 2.2 constant_dynamic-slice_fusion.3
  13.7 0.3 copy.44
  14.0 1.4 copy.45
  15.4 1.2 pad_maximum_fusion
  16.7 0.0 all-gather.4.cloned.1.call-update
  16.7 0.0 all-gather.8.cloned.1.call-start
  16.8 1.0 constant_dynamic-slice_fusion.1
  17.7 0.1 copy.46
  17.9 0.1 copy.47
  18.0 0.7 pad_maximum_fusion.1
  18.7 0.0 all-gather.8.cloned.1.call-update
  18.8 0.0 copy-start.6
  18.8 0.0 copy-start.5
  18.8 0.0 all-gather.6.cloned.1.call-start
  18.8 150.9 %all-gather.4.cloned.1.call-done = bf16[5120,2,512]{0,2,1:T(8,128)(2,1)} async-done(((bf16[640,2,512]{0,2,1:T(8,128)(2,1)}), bf16[5120,2,512]{0,2,1:T(8,128)(2,1)}) %all-gather.4.cloned.1.call-update) | async-done | bytes 10485776 | tf_op jit(solution)/shard_map/all_gather | solution.py:24
  169.7 15.7 %fusion.1 = bf16[640,2,512]{0,2,1:T(8,128)(2,1)} fusion(bf16[5120,2,512]{0,2,1:T(8,128)(2,1)} %all-gather.4.cloned.1.call-done, bf16[2,640,5120]{2,1,0:T(8,128)(2,1)} %param.9), kind=kOutput, calls=%fused_computation.3 | convolution fusion | flops 6711541760 | bytes 24903680 | tf_op jit(solution)/shard_map/jsk,kjn->sjn/dot_general | solution.py:25
  185.4 0.0 all-gather.6.cloned.1.call-update
  185.6 0.6 dynamic-slice
  186.8 33.5 %all-gather.8.cloned.1.call-done = bf16[1024,2,512]{0,2,1:T(8,128)(2,1)} async-done(((bf16[128,2,512]{0,2,1:T(8,128)(2,1)}), bf16[1024,2,512]{0,2,1:T(8,128)(2,1)}) %all-gather.8.cloned.1.call-update) | async-done | bytes 2097168 | tf_op jit(solution)/shard_map/all_gather | solution.py:35
  220.3 2.3 fusion.2
  222.6 1.5 collective-permute-start.1
  224.1 3.3 collective-permute-start
  227.4 1.8 fusion.16
  229.2 11.9 %collective-permute-done.1 = bf16[128,2,512]{0,2,1:T(8,128)(2,1)S(1)} collective-permute-done((bf16[128,2,512]{0,2,1:T(8,128)(2,1)S(1)}, bf16[128,2,512]{0,2,1:T(8,128)(2,1)S(1)}, u32[]{:S(2)}, u32[]{:S(2)}) %collective-permute-start.1) | collective-permute-done | bytes 262176 | tf_op jit(solution)/shard_map/ppermute | solution.py:52
  241.1 2.5 collective-permute-start.3
  243.5 0.0 collective-permute-done
  243.5 2.2 collective-permute-start.2
  245.8 1.8 fusion.12
  247.6 1.8 fusion.14
  249.4 11.0 %collective-permute-done.3 = bf16[128,2,512]{0,2,1:T(8,128)(2,1)S(1)} collective-permute-done((bf16[128,2,512]{0,2,1:T(8,128)(2,1)S(1)}, bf16[128,2,512]{0,2,1:T(8,128)(2,1)S(1)}, u32[]{:S(2)}, u32[]{:S(2)}) %collective-permute-start.3) | collective-permute-done | bytes 262176 | tf_op jit(solution)/shard_map/ppermute | solution.py:52
  260.4 2.5 collective-permute-start.5
  262.8 0.7 collective-permute-done.2
  263.5 1.6 collective-permute-start.4
  265.1 1.8 fusion.10
  266.9 1.8 fusion.8
  268.6 7.4 %collective-permute-done.5 = bf16[128,2,512]{0,2,1:T(8,128)(2,1)S(1)} collective-permute-done((bf16[128,2,512]{0,2,1:T(8,128)(2,1)S(1)}, bf16[128,2,512]{0,2,1:T(8,128)(2,1)S(1)}, u32[]{:S(2)}, u32[]{:S(2)}) %collective-permute-start.5) | collective-permute-done | bytes 262176 | tf_op jit(solution)/shard_map/ppermute | solution.py:52
  276.1 0.0 collective-permute-start.6
  276.1 1.8 fusion.4
  277.8 0.0 collective-permute-done.4
  277.8 1.8 fusion.6
  279.6 108.0 %all-gather.6.cloned.1.call-done = bf16[5120,2,512]{0,2,1:T(8,128)(2,1)} async-done(((bf16[640,2,512]{0,2,1:T(8,128)(2,1)}), bf16[5120,2,512]{0,2,1:T(8,128)(2,1)}) %all-gather.6.cloned.1.call-update) | async-done | bytes 10485776 | tf_op jit(solution)/shard_map/all_gather | solution.py:32
  387.6 12.5 %fusion.27 = f32[2,512,512]{2,1,0:T(8,128)} fusion(bf16[5120,2,512]{0,2,1:T(8,128)(2,1)} %all-gather.6.cloned.1.call-done, bf16[2,512,5120]{2,1,0:T(8,128)(2,1)} %param.7), kind=kOutput, calls=%fused_computation.38 | convolution fusion | flops 5368709120 | bytes 23068672 | tf_op jit(solution)/shard_map/jti,ijn->jtn/dot_general | solution.py:29
  400.1 0.0 collective-permute-done.6
  400.2 5.2 %fusion = f32[512,512]{0,1:T(8,128)S(1)} fusion(f32[2,512,512]{2,1,0:T(8,128)} %fusion.27, f32[2,512,512]{1,2,0:T(8,128)} %fusion.4, f32[2,512,512]{1,2,0:T(8,128)} %fusion.6, f32[2,512,512]{1,2,0:T(8,128)} %fusion.8, f32[2,512,512]{1,2,0:T(8,128)S(1)} %copy-done.4, f32[2,512,512]{1,2,0:T(8,128)S(1)} %copy-done.2, f32[2,512,512]{1,2,0:T(8,128)S(1)} %copy-done.1, ...), kind=kOutput, calls=%fused_computation.1 | convolution fusion | flops 138674176 | bytes 18350084 | tf_op jit(solution)/shard_map/jti,ijn->jtn/dot_general | solution.py:63
  405.3 0.2 bitcast_reduce_fusion
  405.5 10.3 %all-reduce = f32[512,16]{0,1:T(8,128)S(1)} all-reduce(f32[512,16]{0,1:T(8,128)S(1)} %bitcast_reduce_fusion), channel_id=2, replica_groups=mesh['layer'=4,'shard'=8] {'layer'}, use_global_device_ids=true, to_apply=%region_2.3.clone | all-reduce | flops 8192 | bytes 65536
  415.9 0.6 constant_dynamic-slice_fusion.4
  (13 shorter events, 0.0 us)
Async XLA Ops:
  6.5 220.9 %copy-start = (bf16[2,512,1024]{2,1,0:T(8,128)(2,1)S(1)}, bf16[2,512,1024]{2,1,0:T(8,128)(2,1)}, u32[]{:S(2)}) copy-start(bf16[2,512,1024]{2,1,0:T(8,128)(2,1)} %param.8) | copy-start | bytes 6291460
  6.5 163.2 %all-gather.4.cloned.1.call-start = ((), (), s32[]{:S(2)}) async-start(), calls=%async_computation | async-start | bytes 11796480 | tf_op jit(solution)/shard_map/all_gather | solution.py:24
  16.7 203.6 %all-gather.8.cloned.1.call-start = ((), (), s32[]{:S(2)}) async-start(), calls=%async_computation.2 | async-start | bytes 2359296 | tf_op jit(solution)/shard_map/all_gather | solution.py:35
  18.8 166.8 %copy-start.6 = (u32[32]{0:T(128)S(1)}, u32[32]{0:T(128)}, u32[]{:S(2)}) copy-start(u32[32]{0:T(128)} %constant.87) | copy-start | bytes 388
  18.8 201.5 %copy-start.5 = (bf16[2,128,1024]{2,1,0:T(8,128)(2,1)S(1)}, bf16[2,128,1024]{2,1,0:T(8,128)(2,1)}, u32[]{:S(2)}) copy-start(bf16[2,128,1024]{2,1,0:T(8,128)(2,1)} %param.10) | copy-start | bytes 1572868
  18.8 368.9 %all-gather.6.cloned.1.call-start = ((), (), s32[]{:S(2)}) async-start(), calls=%async_computation.1 | async-start | bytes 11796480 | tf_op jit(solution)/shard_map/all_gather | solution.py:32
  222.6 18.4 %collective-permute-start.1 = (bf16[128,2,512]{0,2,1:T(8,128)(2,1)S(1)}, bf16[128,2,512]{0,2,1:T(8,128)(2,1)S(1)}, u32[]{:S(2)}, u32[]{:S(2)}) collective-permute-start(bf16[128,2,512]{0,2,1:T(8,128)(2,1)S(1)} %fusion.2), channel_id=1, source_target_pairs={{0,1},{1,2},{2,3},{3,4},{4,5},{5,6},{6,7},{7,0},{8,9},{9,10},{10,1... | collective-permute-start | bytes 786440 | tf_op jit(solution)/shard_map/ppermute | solution.py:52
  224.1 19.4 %collective-permute-start = (bf16[128,2,512]{0,2,1:T(8,128)(2,1)S(1)}, bf16[128,2,512]{0,2,1:T(8,128)(2,1)S(1)}, u32[]{:S(2)}, u32[]{:S(2)}) collective-permute-start(bf16[128,2,512]{0,2,1:T(8,128)(2,1)S(1)} %fusion.2), channel_id=1, source_target_pairs={{0,7},{1,0},{2,1},{3,2},{4,3},{5,4},{6,5},{7,6},{8,15},{9,8},{10,9... | collective-permute-start | bytes 786440 | tf_op jit(solution)/shard_map/ppermute | solution.py:54
  241.1 19.3 %collective-permute-start.3 = (bf16[128,2,512]{0,2,1:T(8,128)(2,1)S(1)}, bf16[128,2,512]{0,2,1:T(8,128)(2,1)S(1)}, u32[]{:S(2)}, u32[]{:S(2)}) collective-permute-start(bf16[128,2,512]{0,2,1:T(8,128)(2,1)S(1)} %collective-permute-done.1), channel_id=1, source_target_pairs={{0,1},{1,2},{2,3},{3,4},{4,5},{5,6},{6,7},{7,0},{8,9},{9,10},{10,1... | collective-permute-start | bytes 786440 | tf_op jit(solution)/shard_map/ppermute | solution.py:52
  243.5 19.9 %collective-permute-start.2 = (bf16[128,2,512]{0,2,1:T(8,128)(2,1)S(1)}, bf16[128,2,512]{0,2,1:T(8,128)(2,1)S(1)}, u32[]{:S(2)}, u32[]{:S(2)}) collective-permute-start(bf16[128,2,512]{0,2,1:T(8,128)(2,1)S(1)} %collective-permute-done), channel_id=1, source_target_pairs={{0,7},{1,0},{2,1},{3,2},{4,3},{5,4},{6,5},{7,6},{8,15},{9,8},{10,9... | collective-permute-start | bytes 786440 | tf_op jit(solution)/shard_map/ppermute | solution.py:54
  260.4 15.7 %collective-permute-start.5 = (bf16[128,2,512]{0,2,1:T(8,128)(2,1)S(1)}, bf16[128,2,512]{0,2,1:T(8,128)(2,1)S(1)}, u32[]{:S(2)}, u32[]{:S(2)}) collective-permute-start(bf16[128,2,512]{0,2,1:T(8,128)(2,1)S(1)} %collective-permute-done.3), channel_id=1, source_target_pairs={{0,1},{1,2},{2,3},{3,4},{4,5},{5,6},{6,7},{7,0},{8,9},{9,10},{10,1... | collective-permute-start | bytes 786440 | tf_op jit(solution)/shard_map/ppermute | solution.py:52
  263.5 14.4 %collective-permute-start.4 = (bf16[128,2,512]{0,2,1:T(8,128)(2,1)S(1)}, bf16[128,2,512]{0,2,1:T(8,128)(2,1)S(1)}, u32[]{:S(2)}, u32[]{:S(2)}) collective-permute-start(bf16[128,2,512]{0,2,1:T(8,128)(2,1)S(1)} %collective-permute-done.2), channel_id=1, source_target_pairs={{0,7},{1,0},{2,1},{3,2},{4,3},{5,4},{6,5},{7,6},{8,15},{9,8},{10,9... | collective-permute-start | bytes 786440 | tf_op jit(solution)/shard_map/ppermute | solution.py:54
  276.1 124.1 %collective-permute-start.6 = (bf16[128,2,512]{0,2,1:T(8,128)(2,1)S(1)}, bf16[128,2,512]{0,2,1:T(8,128)(2,1)S(1)}, u32[]{:S(2)}, u32[]{:S(2)}) collective-permute-start(bf16[128,2,512]{0,2,1:T(8,128)(2,1)S(1)} %collective-permute-done.5), channel_id=1, source_target_pairs={{0,1},{1,2},{2,3},{3,4},{4,5},{5,6},{6,7},{7,0},{8,9},{9,10},{10,1... | collective-permute-start | bytes 786440 | tf_op jit(solution)/shard_map/ppermute | solution.py:52
  387.6 12.5 %copy-start.1 = (f32[2,512,512]{1,2,0:T(8,128)S(1)}, f32[2,512,512]{1,2,0:T(8,128)}, u32[]{:S(2)}) copy-start(f32[2,512,512]{1,2,0:T(8,128)} %fusion.16) | copy-start | bytes 6291460
  387.6 12.5 %copy-start.2 = (f32[2,512,512]{1,2,0:T(8,128)S(1)}, f32[2,512,512]{1,2,0:T(8,128)}, u32[]{:S(2)}) copy-start(f32[2,512,512]{1,2,0:T(8,128)} %fusion.12) | copy-start | bytes 6291460
  387.6 12.5 %copy-start.3 = (f32[2,512,512]{1,2,0:T(8,128)S(1)}, f32[2,512,512]{1,2,0:T(8,128)}, u32[]{:S(2)}) copy-start(f32[2,512,512]{1,2,0:T(8,128)} %fusion.14) | copy-start | bytes 6291460
  387.6 12.5 %copy-start.4 = (f32[2,512,512]{1,2,0:T(8,128)S(1)}, f32[2,512,512]{1,2,0:T(8,128)}, u32[]{:S(2)}) copy-start(f32[2,512,512]{1,2,0:T(8,128)} %fusion.10) | copy-start | bytes 6291460
Sparse Core Ops, SparseCore 0:
  16.8 152.8 all-gather.3
  171.7 48.5 all-gather.7
  222.5 165.0 all-gather.5
